TPU v7x, 32 devices: a whole 2x2x4 slice. The times are simulated.
32 devices in a mesh: sec: 4 (over y, x), seq: 8 (over z, core).
Axes of the slice: x: 2, y: 2, z: 4, core: 2. Of those that a mesh axis runs over, the one named last changes fastest.
Arguments:
- long_queries: bfloat16 [16, 4096], P('sec'), may hold values from -15 to 15
- long_keys: bfloat16 [512, 16, 2048], P(('sec', 'seq')), may hold values from -6 to 6
- long_values: bfloat16 [512, 16, 2048], P(('sec', 'seq')), may hold values from -6 to 6
- page_table: int32 [16, 32], replicated, may hold values from 0 to 511, as said below
- long_lengths: int32 [16], replicated, may hold values from 1 to 512, 5120 in all
- short_queries: bfloat16 [32, 256], P(('sec', 'seq')), may hold values from -15 to 15
- short_keys: bfloat16 [32, 2048, 128], P(('sec', 'seq')), may hold values from -6 to 6
- short_values: bfloat16 [32, 2048, 128], P(('sec', 'seq')), may hold values from -6 to 6
- short_lengths: int32 [2], replicated, may hold values from 1 to 2048, 2560 in all
- out_weight: bfloat16 [4096, 4608], P('seq', 'sec'), may hold values from -0.09375 to 0.09375
- long_resid: bfloat16 [16, 4608], P(None, 'sec'), may hold values from -1.5 to 1.5
Outputs:
- long_out: bfloat16 [16, 4608], P(None, 'sec')
- short_out: bfloat16 [32, 256], P(('sec', 'seq'))
Inputs may be any that keep to these rules, and one draw needn't show every extreme that they name: `page_table`: row r lists the 32 pool pages of long request r in order of position; every page of the pool of 512 appears exactly once; page g is held by device g // 16 along sec+seq. `long_lengths`: counts the newest token; later slots are unused. `short_lengths`: counts the newest token; later slots are unused.
All inputs are finite; a program needn't handle non-finite values.
Results may differ from a plain program's by a relative error of at most 0.0055.
Values may be sent and summed in bfloat16 or wider, within the bound.
A program may use at most 64 MiB of HBM per device.

v0:
```python
import jax
import jax.numpy as jnp
from jax import lax
from jax.sharding import PartitionSpec as P

KVH = 16
HD = 128
G = 2
soft_cap = 50.0
score_scale = 144.0 ** (-0.5)


def capped_weights(raw_scores, live_mask):
    capped = soft_cap * jnp.tanh(raw_scores * (score_scale / soft_cap))
    return jnp.where(live_mask, jnp.exp(capped), 0.0)


def per_device(
    long_queries,
    long_keys,
    long_values,
    page_table,
    long_lengths,
    short_queries,
    short_keys,
    short_values,
    short_lengths,
    out_weight,
    long_resid,
):
    queries = lax.all_gather(long_queries, "sec", axis=0, tiled=True)
    requests = queries.shape[0]
    page_count, page_len, kv_width = long_keys.shape
    tokens = page_count * page_len
    head_count = KVH * G
    first_page = lax.axis_index(("sec", "seq")) * page_count
    page_ids = first_page + jnp.arange(page_count, dtype=jnp.int32)
    matched = page_table[:, :, None] == page_ids[None, None, :]
    page_held = jnp.any(matched, axis=1)
    slot_index = jnp.arange(page_table.shape[1], dtype=jnp.int32)
    slot_of = jnp.sum(jnp.where(matched, slot_index[None, :, None], 0), axis=1)
    position = slot_of[:, :, None] * page_len + jnp.arange(page_len, dtype=jnp.int32)[None, None, :]
    live_mask = page_held[:, :, None] & (position < long_lengths[:, None, None])
    live_mask = live_mask.reshape(requests, tokens)
    grouped = (
        queries.reshape(requests, KVH, G, HD).transpose(1, 0, 2, 3).reshape(KVH, requests * G, HD)
    )
    key_rows = long_keys.reshape(tokens, KVH, HD)
    value_rows = long_values.reshape(tokens, KVH, HD)
    raw_scores = jnp.einsum("hqd,thd->hqt", grouped, key_rows, preferred_element_type=jnp.float32)
    token_mask = jnp.broadcast_to(live_mask[None, :, None, :], (KVH, requests, G, tokens)).reshape(
        KVH, requests * G, tokens
    )
    weights = capped_weights(raw_scores, token_mask)
    totals = jnp.sum(weights, axis=2)
    part_sums = jnp.einsum(
        "hqt,thd->hqd", weights.astype(jnp.bfloat16), value_rows, preferred_element_type=jnp.float32
    )
    part_sums = (
        part_sums.reshape(KVH, requests, G, HD)
        .transpose(1, 0, 2, 3)
        .reshape(requests, head_count * HD)
    )
    totals = totals.reshape(KVH, requests, G).transpose(1, 0, 2).reshape(requests, head_count)
    share_width = out_weight.shape[0]
    share_start = lax.axis_index("seq") * share_width
    part_sums, totals = lax.psum((part_sums, totals), ("sec", "seq"))
    attention = (
        (part_sums.reshape(requests, head_count, HD) / totals[:, :, None])
        .astype(jnp.bfloat16)
        .reshape(requests, head_count * HD)
    )
    feature_rows = lax.dynamic_slice_in_dim(attention, share_start, share_width, 1)
    partial_proj = jnp.dot(feature_rows, out_weight, preferred_element_type=jnp.float32)
    projected = lax.psum(partial_proj, "seq")
    long_out = (long_resid.astype(jnp.float32) + projected).astype(jnp.bfloat16)
    pair_count = short_queries.shape[0]
    length = short_keys.shape[1]
    pair_ids = lax.axis_index(("sec", "seq")) * pair_count + jnp.arange(pair_count, dtype=jnp.int32)
    request_of = pair_ids // KVH
    chosen = request_of[:, None] == jnp.arange(short_lengths.shape[0], dtype=jnp.int32)[None, :]
    pair_limit = jnp.sum(jnp.where(chosen, short_lengths[None, :], 0), axis=1)
    short_live = jnp.arange(length, dtype=jnp.int32)[None, :] < pair_limit[:, None]
    pair_queries = short_queries.reshape(pair_count, G, HD)
    short_scores = jnp.einsum(
        "pgd,ptd->pgt", pair_queries, short_keys, preferred_element_type=jnp.float32
    )
    short_weights = capped_weights(short_scores, short_live[:, None, :])
    short_totals = jnp.sum(short_weights, axis=2)
    short_sums = jnp.einsum(
        "pgt,ptd->pgd",
        short_weights.astype(jnp.bfloat16),
        short_values,
        preferred_element_type=jnp.float32,
    )
    short_out = (
        (short_sums / short_totals[:, :, None]).astype(jnp.bfloat16).reshape(pair_count, G * HD)
    )
    return (long_out, short_out)


def solution(mesh):
    in_specs = (
        P("sec", None),
        P(("sec", "seq"), None, None),
        P(("sec", "seq"), None, None),
        P(),
        P(),
        P(("sec", "seq"), None),
        P(("sec", "seq"), None, None),
        P(("sec", "seq"), None, None),
        P(),
        P("seq", "sec"),
        P(None, "sec"),
    )
    out_specs = (P(None, "sec"), P(("sec", "seq"), None))
    return jax.shard_map(
        per_device, mesh=mesh, in_specs=in_specs, out_specs=out_specs, check_vma=False
    )
```

profile of v0, /device:TPU:8, one launch (start us, length us, event | category | flops | bytes accessed | tf_op | source)
XLA Modules:
  0.0 212.9 jit_solution(14925022806387552283)
XLA Ops:
  7.2 1.2 fusion.16
  8.4 1.1 compare_reduce_fusion
  9.6 0.1 add.56
  9.7 0.1 add.57
  9.8 0.1 and.21
  9.9 0.1 and.22
  10.0 0.1 add.59
  10.1 0.7 fusion.20
  10.9 1.5 copy.36
  12.5 8.5 %all-gather = bf16[4,4,4096]{2,1,0:T(4,128)(2,1)S(1)} all-gather(bf16[1,4,4096]{2,1,0:T(4,128)(2,1)S(1)} %bitcast.58), channel_id=1, replica_groups=mesh['sec'=4,'seq'=8] {'sec'}, dimensions={0}, use_global_device_ids=true | all-gather | bytes 163840 | tf_op jit(solution)/shard_map/all_gather | solution.py:31
  20.9 0.2 reshape.129
  21.1 0.1 copy.29
  21.2 0.2 copy.37
  21.4 0.6 fusion.25
  22.0 0.3 fusion.10
  22.4 0.1 copy.50
  22.5 0.9 reshape.134
  23.5 0.6 fusion.22
  24.2 0.7 iota_compare_fusion
  24.8 0.1 copy.33
  24.9 0.1 copy.34
  25.0 39.6 %psum.22 = f32[16,32]{0,1:T(8,128)S(1)} all-reduce(f32[16,32]{0,1:T(8,128)S(1)} %bitcast.57), channel_id=1, replica_groups=mesh['sec'=4,'seq'=8] {'sec','seq'}, use_global_device_ids=true, to_apply=%region_4.5 | all-reduce | flops 512 | bytes 4096 | tf_op jit(solution)/shard_map/psum | solution.py:67
  64.6 0.1 copy.35
  64.7 0.1 div.30
  64.8 0.2 copy.49
  65.0 0.4 fusion.26
  65.4 85.0 %all-reduce.3.cloned.1.call-done = f32[16,4096]{1,0:T(8,128)} async-done(((f32[16,4096]{1,0:T(8,128)}), f32[16,4096]{1,0:T(8,128)}) %all-reduce.3.cloned.1.call-update) | async-done | bytes 262160 | tf_op jit(solution)/shard_map/psum | solution.py:67
  150.4 1.6 fusion.18
  152.1 0.2 fusion.9
  152.3 0.6 copy.51
  152.9 51.7 %all-reduce.5.cloned.1.call-done = f32[16,1152]{1,0:T(8,128)} async-done(((f32[16,1152]{1,0:T(8,128)}), f32[16,1152]{1,0:T(8,128)}) %all-reduce.5.cloned.1.call-update) | async-done | bytes 73744 | tf_op jit(solution)/shard_map/psum | solution.py:75
  204.5 1.5 add_convert_fusion
  (26 shorter events, 0.2 us)
Async XLA Ops:
  7.2 143.3 %copy-start = (bf16[512,1152]{1,0:T(8,128)(2,1)S(1)}, bf16[512,1152]{1,0:T(8,128)(2,1)}, u32[]{:S(2)}) copy-start(bf16[512,1152]{1,0:T(8,128)(2,1)} %param.20) | copy-start | bytes 3538948
  7.2 143.2 %all-reduce.3.cloned.1.call-start = ((), (), s32[]{:S(2)}) async-start(), calls=%async_computation | async-start | bytes 524288 | tf_op jit(solution)/shard_map/psum | solution.py:67
  9.7 2.8 %copy-start.4 = (bf16[4,4096]{1,0:T(4,128)(2,1)S(1)}, bf16[4,4096]{1,0:T(4,128)(2,1)}, u32[]{:S(2)}) copy-start(bf16[4,4096]{1,0:T(4,128)(2,1)} %param.11) | copy-start | bytes 98308
  10.9 10.3 %copy-start.1 = (bf16[16,16,2048]{2,1,0:T(8,128)(2,1)S(1)}, bf16[16,16,2048]{2,1,0:T(8,128)(2,1)}, u32[]{:S(2)}) copy-start(bf16[16,16,2048]{2,1,0:T(8,128)(2,1)} %param.13) | copy-start | bytes 3145732
  22.0 1.5 copy-start.7
  22.4 42.6 %copy-start.5 = (bf16[1,256]{1,0:T(2,128)(2,1)S(1)}, bf16[1,256]{1,0:T(2,128)(2,1)}, u32[]{:S(2)}) copy-start(bf16[1,256]{1,0:T(2,128)(2,1)} %param.16) | copy-start | bytes 1540
  22.4 42.6 %copy-start.2 = (bf16[1,2048,128]{2,1,0:T(8,128)(2,1)S(1)}, bf16[1,2048,128]{2,1,0:T(8,128)(2,1)}, u32[]{:S(2)}) copy-start(bf16[1,2048,128]{2,1,0:T(8,128)(2,1)} %param.17) | copy-start | bytes 1572868
  23.5 181.1 %all-reduce.5.cloned.1.call-start = ((), (), s32[]{:S(2)}) async-start(), calls=%async_computation.1 | async-start | bytes 147456 | tf_op jit(solution)/shard_map/psum | solution.py:75
  64.8 87.3 %copy-start.6 = (bf16[1,2048,128]{2,1,0:T(8,128)(2,1)S(1)}, bf16[1,2048,128]{2,1,0:T(8,128)(2,1)}, u32[]{:S(2)}) copy-start(bf16[1,2048,128]{2,1,0:T(8,128)(2,1)} %param.18) | copy-start | bytes 1572868
  65.0 139.5 %copy-start.3 = (bf16[16,1152]{1,0:T(8,128)(2,1)S(1)}, bf16[16,1152]{1,0:T(8,128)(2,1)}, u32[]{:S(2)}) copy-start(bf16[16,1152]{1,0:T(8,128)(2,1)} %param.21) | copy-start | bytes 110596
Sparse Core Ops, SparseCore 0:
  23.6 126.7 all-reduce.2
  152.8 51.7 all-reduce.4
where the time goes:
time: 213 us
  waiting for transfers between devices  137 us (64%)
  blocking collectives  48.1 us (23%)
  between operations  14.3 us (7%)
  other arithmetic  5.86 us (3%)
  local copies, waits for them, and re-layouts  4.75 us (2%)
  matrix products  3.13 us (1%)
    psum x1, waiting for transfers between devices, per_device(): part_sums, totals = lax.psum((part_sums, totals), ('sec', 'seq'))  85 us
    psum x1, waiting for transfers between devices, per_device(): projected = lax.psum(partial_proj, 'seq')  51.7 us
    psum x1, blocking collectives, per_device(): part_sums, totals = lax.psum((part_sums, totals), ('sec', 'seq'))  39.6 us
    all_gather x1, blocking collectives, per_device(): queries = lax.all_gather(long_queries, 'sec', axis=0, tiled=True)  8.46 us
  transfers between devices with their start and end apart: 2, of which 2 were waited for; matrix products, arithmetic and copies ran while one was open for 1% of the time, Pallas kernels for 0%

commit v1 on v0

--- a/solution.py
+++ b/solution.py
@@ -72,7 +72,11 @@
     )
     feature_rows = lax.dynamic_slice_in_dim(attention, share_start, share_width, 1)
     partial_proj = jnp.dot(feature_rows, out_weight, preferred_element_type=jnp.float32)
-    projected = lax.psum(partial_proj, "seq")
+    projected = partial_proj
+    for hop in (1, 2, 4):
+        projected = projected + lax.ppermute(
+            projected, "seq", [(dev, dev ^ hop) for dev in range(8)]
+        )
     long_out = (long_resid.astype(jnp.float32) + projected).astype(jnp.bfloat16)
     pair_count = short_queries.shape[0]
     length = short_keys.shape[1]

time: 213 us -> 172 us (0.81)
  waiting for transfers between devices: 137 us -> 93.4 us
    psum x1 -> x0, waiting for transfers between devices: 51.7 us -> none  [per_device(): projected = lax.psum(partial_proj, 'seq')]
    ppermute x0 -> x3, waiting for transfers between devices: none -> 7.07 us  [per_device(): lax.ppermute(projected, 'seq', [(dev, dev ^ hop) for dev in range(8)])]
    ppermute x0 -> x3, starting transfers between devices: none -> 2.14 us  [per_device(): lax.ppermute(projected, 'seq', [(dev, dev ^ hop) for dev in range(8)])]
  transfers between devices with their start and end apart: 2 -> 4, of which waited for: 2 -> 4; matrix products, arithmetic and copies ran while one was open for 1% -> 2% of each run, Pallas kernels for 0% -> 0%
where the time goes in v1:
time: 172 us; the launch traced here: 170 us
  waiting for transfers between devices  93.4 us (54%)
  blocking collectives  47.9 us (28%)
  between operations  14.3 us (8%)
  other arithmetic  5.01 us (3%)
  local copies, waits for them, and re-layouts  4.75 us (3%)
  matrix products  2.5 us (1%)
  starting transfers between devices  2.18 us (1%)
    psum x1, waiting for transfers between devices, per_device(): part_sums, totals = lax.psum((part_sums, totals), ('sec', 'seq'))  86.3 us
    psum x1, blocking collectives, per_device(): part_sums, totals = lax.psum((part_sums, totals), ('sec', 'seq'))  39.5 us
    all_gather x1, blocking collectives, per_device(): queries = lax.all_gather(long_queries, 'sec', axis=0, tiled=True)  8.46 us
    ppermute x3, waiting for transfers between devices, per_device(): lax.ppermute(projected, 'seq', [(dev, dev ^ hop) for dev in range(8)])  7.07 us
  transfers between devices with their start and end apart: 4, of which 4 were waited for; matrix products, arithmetic and copies ran while one was open for 2% of the time, Pallas kernels for 0%

profile of v1, /device:TPU:8, one launch (start us, length us, event | category | flops | bytes accessed | tf_op | source)
XLA Modules:
  0.0 170.0 jit_solution(15663106101753935062)
XLA Ops:
  7.2 1.2 fusion.16
  8.4 1.1 compare_reduce_fusion
  9.6 0.1 add.63
  9.7 0.1 add.64
  9.8 0.1 and.21
  9.9 0.1 and.22
  10.1 0.7 fusion.20
  10.9 1.5 copy.36
  12.5 8.5 %all-gather = bf16[4,4,4096]{2,1,0:T(4,128)(2,1)S(1)} all-gather(bf16[1,4,4096]{2,1,0:T(4,128)(2,1)S(1)} %bitcast.58), channel_id=1, replica_groups=mesh['sec'=4,'seq'=8] {'sec'}, dimensions={0}, use_global_device_ids=true | all-gather | bytes 163840 | tf_op jit(solution)/shard_map/all_gather | solution.py:31
  20.9 0.2 reshape.129
  21.1 0.1 copy.29
  21.2 0.2 copy.37
  21.4 0.6 fusion.25
  22.0 0.3 fusion.10
  22.4 0.1 copy.50
  22.5 0.9 reshape.134
  23.6 39.5 %psum.15 = f32[16,32]{0,1:T(8,128)S(1)} all-reduce(f32[16,32]{0,1:T(8,128)S(1)} %bitcast.57), channel_id=1, replica_groups=mesh['sec'=4,'seq'=8] {'sec','seq'}, use_global_device_ids=true, to_apply=%region_4.5 | all-reduce | flops 512 | bytes 4096 | tf_op jit(solution)/shard_map/psum | solution.py:67
  63.2 0.1 div.30
  63.3 0.2 copy.49
  63.6 0.6 fusion.22
  64.2 86.3 %all-reduce.2.cloned.1.call-done = f32[16,4096]{1,0:T(8,128)} async-done(((f32[16,4096]{1,0:T(8,128)}), f32[16,4096]{1,0:T(8,128)}) %all-reduce.2.cloned.1.call-update) | async-done | bytes 262160 | tf_op jit(solution)/shard_map/psum | solution.py:67
  150.5 1.0 fusion.18
  151.5 0.7 iota_compare_fusion
  152.2 0.6 collective-permute-done
  152.8 0.6 collective-permute-start.1
  153.4 0.4 fusion.26
  153.8 3.4 %collective-permute-done.1 = f32[16,1152]{1,0:T(8,128)S(1)} collective-permute-done((f32[16,1152]{1,0:T(8,128)S(1)}, f32[16,1152]{1,0:T(8,128)S(1)}, u32[]{:S(2)}, u32[]{:S(2)}) %collective-permute-start.1) | collective-permute-done | bytes 73760 | tf_op jit(solution)/shard_map/ppermute | solution.py:77
  157.2 1.5 collective-permute-start.2
  158.7 0.2 fusion.9
  158.9 0.6 copy.51
  159.5 3.0 %collective-permute-done.2 = f32[16,1152]{1,0:T(8,128)S(1)} collective-permute-done((f32[16,1152]{1,0:T(8,128)S(1)}, f32[16,1152]{1,0:T(8,128)S(1)}, u32[]{:S(2)}, u32[]{:S(2)}) %collective-permute-start.2) | collective-permute-done | bytes 73760 | tf_op jit(solution)/shard_map/ppermute | solution.py:77
  162.5 0.6 add_convert_fusion
  (31 shorter events, 0.5 us)
Async XLA Ops:
  7.2 143.3 %copy-start = (bf16[512,1152]{1,0:T(8,128)(2,1)S(1)}, bf16[512,1152]{1,0:T(8,128)(2,1)}, u32[]{:S(2)}) copy-start(bf16[512,1152]{1,0:T(8,128)(2,1)} %param.20) | copy-start | bytes 3538948
  7.2 143.3 %all-reduce.2.cloned.1.call-start = ((), (), s32[]{:S(2)}) async-start(), calls=%async_computation | async-start | bytes 524288 | tf_op jit(solution)/shard_map/psum | solution.py:67
  9.7 2.8 %copy-start.4 = (bf16[4,4096]{1,0:T(4,128)(2,1)S(1)}, bf16[4,4096]{1,0:T(4,128)(2,1)}, u32[]{:S(2)}) copy-start(bf16[4,4096]{1,0:T(4,128)(2,1)} %param.11) | copy-start | bytes 98308
  10.9 10.3 %copy-start.1 = (bf16[16,16,2048]{2,1,0:T(8,128)(2,1)S(1)}, bf16[16,16,2048]{2,1,0:T(8,128)(2,1)}, u32[]{:S(2)}) copy-start(bf16[16,16,2048]{2,1,0:T(8,128)(2,1)} %param.13) | copy-start | bytes 3145732
  22.4 41.1 %copy-start.5 = (bf16[1,256]{1,0:T(2,128)(2,1)S(1)}, bf16[1,256]{1,0:T(2,128)(2,1)}, u32[]{:S(2)}) copy-start(bf16[1,256]{1,0:T(2,128)(2,1)} %param.16) | copy-start | bytes 1540
  22.4 41.2 %copy-start.7 = (s32[2]{0:T(128)S(1)}, s32[2]{0:T(128)}, u32[]{:S(2)}) copy-start(s32[2]{0:T(128)} %param.19) | copy-start | bytes 28
  63.2 90.2 %copy-start.2 = (bf16[1,2048,128]{2,1,0:T(8,128)(2,1)S(1)}, bf16[1,2048,128]{2,1,0:T(8,128)(2,1)}, u32[]{:S(2)}) copy-start(bf16[1,2048,128]{2,1,0:T(8,128)(2,1)} %param.17) | copy-start | bytes 1572868
  63.5 95.2 %copy-start.6 = (bf16[1,2048,128]{2,1,0:T(8,128)(2,1)S(1)}, bf16[1,2048,128]{2,1,0:T(8,128)(2,1)}, u32[]{:S(2)}) copy-start(bf16[1,2048,128]{2,1,0:T(8,128)(2,1)} %param.18) | copy-start | bytes 1572868
  150.5 12.1 %copy-start.3 = (bf16[16,1152]{1,0:T(8,128)(2,1)S(1)}, bf16[16,1152]{1,0:T(8,128)(2,1)}, u32[]{:S(2)}) copy-start(bf16[16,1152]{1,0:T(8,128)(2,1)} %param.21) | copy-start | bytes 110596
  151.5 1.3 collective-permute-start
  152.8 4.4 %collective-permute-start.1 = (f32[16,1152]{1,0:T(8,128)S(1)}, f32[16,1152]{1,0:T(8,128)S(1)}, u32[]{:S(2)}, u32[]{:S(2)}) collective-permute-start(f32[16,1152]{1,0:T(8,128)S(1)} %add.70), channel_id=1, source_target_pairs={{0,2},{1,3},{2,0},{3,1},{4,6},{5,7},{6,4},{7,5},{8,10},{9,11},{10,... | collective-permute-start | bytes 221192 | tf_op jit(solution)/shard_map/ppermute | solution.py:77
  157.2 5.3 %collective-permute-start.2 = (f32[16,1152]{1,0:T(8,128)S(1)}, f32[16,1152]{1,0:T(8,128)S(1)}, u32[]{:S(2)}, u32[]{:S(2)}) collective-permute-start(f32[16,1152]{1,0:T(8,128)S(1)} %add.71), channel_id=1, source_target_pairs={{0,4},{1,5},{2,6},{3,7},{4,0},{5,1},{6,2},{7,3},{8,12},{9,13},{10,... | collective-permute-start | bytes 221192 | tf_op jit(solution)/shard_map/ppermute | solution.py:77
Sparse Core Ops, SparseCore 0:
  23.6 126.8 all-reduce.1
